TPU v7x, 32 devices: a whole 2x2x4 slice. The times are simulated.
32 devices in a mesh: grp: 1, col: 32 (over z, y, x, core).
Axes of the slice: x: 2, y: 2, z: 4, core: 2. Of those that a mesh axis runs over, the one named last changes fastest.
Arguments:
- pair: bfloat16 [16, 1024, 128], P('grp', 'col'), may hold values from -6 to 6
- w_query: bfloat16 [128, 128], replicated, may hold values from -0.5 to 0.5
- w_kv: bfloat16 [128, 256], replicated, may hold values from -0.5 to 0.5
- w_gate: bfloat16 [128, 128], replicated, may hold values from -0.5 to 0.5
- w_out: bfloat16 [128, 128], replicated, may hold values from -0.5 to 0.5
- pair_bias: bfloat16 [4, 1024, 1024], P('grp', 'col'), may hold values from -8 to 300
- lengths: int32 [1], P('grp'), may hold values from 512 to 1024
Outputs:
- update: bfloat16 [16, 1024, 128], P('grp', 'col')
All inputs are finite; a program needn't handle non-finite values.
Results may differ from a plain program's by a relative error of at most 0.0081.
Values may be sent and summed in bfloat16 or wider, within the bound.
No kernel may reach another device: no remote copies, remote signals or barrier semaphores. Data moves between devices by JAX's collectives and lax.ppermute only.
A program may use at most 128 MiB of HBM per device.

v0:
```python
import jax
import jax.numpy as jnp
from jax import lax
from jax.sharding import PartitionSpec as P

HEADS = 4


def normalize(pair_block):
    values_f = pair_block.astype(jnp.float32)
    mean_val = jnp.mean(values_f, axis=-1, keepdims=True)
    centred = values_f - mean_val
    variance = jnp.mean(centred * centred, axis=-1, keepdims=True)
    return (centred * lax.rsqrt(variance + 1e-05)).astype(jnp.bfloat16)


def attend(normed, bias_query, key_limit, w_query, w_kv, w_gate, w_out, gather_keys):
    row_count, col_count, chan_count = normed.shape
    head_width = chan_count // HEADS
    queries = (
        jnp.dot(normed, w_query, preferred_element_type=jnp.float32) * head_width ** (-0.5)
    ).astype(jnp.bfloat16)
    queries = queries.reshape(row_count, col_count, HEADS, head_width)
    gate_act = jax.nn.sigmoid(jnp.dot(normed, w_gate, preferred_element_type=jnp.float32))

    def consume(running, segment, offset):
        run_max, run_sum, run_acc = running
        key_value = jnp.dot(segment, w_kv, preferred_element_type=jnp.float32).astype(jnp.bfloat16)
        tile_len = key_value.shape[1]
        key_tile = key_value[:, :, :chan_count].reshape(row_count, tile_len, HEADS, head_width)
        value_tile = key_value[:, :, chan_count:].reshape(row_count, tile_len, HEADS, head_width)
        scores = jnp.einsum(
            "rjhd,rkhd->rhjk", queries, key_tile, preferred_element_type=jnp.float32
        )
        bias_part = lax.dynamic_slice_in_dim(bias_query, offset, tile_len, 2).astype(jnp.float32)
        key_pos = offset + jnp.arange(tile_len, dtype=jnp.int32)
        key_mask = jnp.where(key_pos < key_limit, 0.0, -1000000000.0).astype(jnp.float32)
        scores = scores + bias_part[None] + key_mask
        new_max = jnp.maximum(run_max, jnp.max(scores, axis=-1))
        rescale = jnp.exp(run_max - new_max)
        expon = jnp.exp(scores - new_max[..., None])
        new_sum = run_sum * rescale + jnp.sum(expon, axis=-1)
        weights = expon.astype(jnp.bfloat16)
        partial_out = jnp.einsum(
            "rhjk,rkhd->rjhd", weights, value_tile, preferred_element_type=jnp.float32
        )
        new_acc = run_acc * jnp.transpose(rescale, (0, 2, 1))[..., None] + partial_out
        return (new_max, new_sum, new_acc)

    def fold_piece(running, segment, offset, project):
        tile_len = segment.shape[1]
        block_len = 512
        block_num = tile_len // block_len
        blocks = jnp.moveaxis(
            segment.reshape(row_count, block_num, block_len, segment.shape[2]), 1, 0
        )

        def advance(state_now, item_pair):
            block_tile, block_idx = item_pair
            return (consume(state_now, block_tile, block_idx * block_len), None)

        final_state, unused = lax.scan(
            advance, running, (blocks, jnp.arange(block_num, dtype=jnp.int32))
        )
        return final_state

    initial = (
        jnp.full((row_count, HEADS, col_count), -1e30, jnp.float32),
        jnp.zeros((row_count, HEADS, col_count), jnp.float32),
        jnp.zeros((row_count, col_count, HEADS, head_width), jnp.float32),
    )
    run_max, run_sum, run_acc = gather_keys(fold_piece, initial)
    attended = run_acc / jnp.transpose(run_sum, (0, 2, 1))[..., None]
    hidden = (gate_act * attended.reshape(row_count, col_count, chan_count)).astype(jnp.bfloat16)
    return jnp.dot(hidden, w_out, preferred_element_type=jnp.float32).astype(jnp.bfloat16)


def on_device(pair, w_query, w_kv, w_gate, w_out, pair_bias, lengths):
    key_limit = lengths[0]
    normed = normalize(pair)
    received = lax.all_to_all(pair_bias, "col", split_axis=2, concat_axis=1, tiled=True)
    bias_query = jnp.transpose(received, (0, 2, 1))

    def gather_keys(fold_piece, initial):
        return fold_piece(
            initial, lax.all_gather(normed, "col", axis=1, tiled=True), jnp.int32(0), True
        )

    return attend(normed, bias_query, key_limit, w_query, w_kv, w_gate, w_out, gather_keys)


def solution(mesh):
    in_specs = (P("grp", "col", None), P(), P(), P(), P(), P("grp", "col", None), P("grp"))
    out_specs = P("grp", "col", None)
    return jax.shard_map(
        on_device, mesh=mesh, in_specs=in_specs, out_specs=out_specs, check_vma=False
    )
```

profile of v0, /device:TPU:0, one launch (start us, length us, event | category | flops | bytes accessed | tf_op | source)
XLA Modules:
  0.0 114.1 jit_solution(4545162258831155141)
XLA Ops:
  6.5 0.0 copy-start
  6.5 0.0 all-gather.2.cloned.1.call-start
  6.5 1.1 convert_reduce_fusion
  7.6 1.2 %fusion.30 = f32[16,32]{1,0:T(8,128)S(1)} fusion(bf16[16,32,128]{2,1,0:T(8,128)(2,1)} %param.9, f32[16,32]{1,0:T(8,128)S(1)} %broadcast_multiply_fusion), kind=kLoop, calls=%fused_computation.40 | loop fusion | flops 261632 | bytes 135168 | tf_op jit(solution)/shard_map/reduce_sum | solution.py:13
  8.8 1.8 %fusion.31 = bf16[16,32,128]{2,1,0:T(8,128)(2,1)} fusion(bf16[16,32,128]{2,1,0:T(8,128)(2,1)} %param.9, f32[16,32]{1,0:T(8,128)S(1)} %add_rsqrt_fusion, f32[16,32]{1,0:T(8,128)S(1)} %broadcast_multiply_fusion), kind=kLoop, calls=%fused_computation.41 | loop fusion | flops 262144 | bytes 266240 | tf_op jit(solution)/shard_map/convert_element_type | solution.py:14
  10.6 0.0 all-gather.2.cloned.1.call-update
  10.6 1.6 %copy.17 = bf16[4,32,1024]{1,0,2:T(4,128)(2,1)S(1)} copy(bf16[4,32,1024]{2,1,0:T(8,128)(2,1)} %param.14) | data formatting | bytes 524288 | tf_op args[5]
  12.2 1.7 %reshape.48 = bf16[32,2,2048]{2,1,0:T(2,128)(2,1)} reshape(bf16[1024,4,32]{2,1,0:T(4,128)(2,1)S(1)} %bitcast.92) | data formatting | bytes 524288
  13.9 7.3 %all-to-all-start = ((bf16[32,2,2048]{2,1,0:T(2,128)(2,1)}), bf16[32,2,2048]{2,1,0:T(2,128)(2,1)S(1)}, u32[]{:S(2)}, u32[]{:S(2)}) async-start(bf16[32,2,2048]{2,1,0:T(2,128)(2,1)} %reshape.48), calls=%async_computation | async-start | bytes 524288 | tf_op jit(solution)/shard_map/all_to_all | solution.py:81
  21.3 0.0 copy-done
  21.3 1.1 fusion.27
  22.4 0.2 reshape.40
  22.6 0.9 copy.21
  23.5 0.0 copy-done.5
  23.5 0.7 copy.20
  24.3 8.9 %all-to-all-done = bf16[32,2,2048]{2,1,0:T(2,128)(2,1)S(1)} async-done(((bf16[32,2,2048]{2,1,0:T(2,128)(2,1)}), bf16[32,2,2048]{2,1,0:T(2,128)(2,1)S(1)}, u32[]{:S(2)}, u32[]{:S(2)}) %all-to-all-start) | async-done | bytes 262176 | tf_op jit(solution)/shard_map/all_to_all | solution.py:81
  33.2 0.5 reshape.49
  33.7 0.7 copy.18
  34.4 1.1 all_to_all.16
  35.5 42.7 %all-gather.2.cloned.1.call-done = bf16[16,1024,128]{2,1,0:T(8,128)(2,1)} async-done(((bf16[16,32,128]{2,1,0:T(8,128)(2,1)}), bf16[16,1024,128]{2,1,0:T(8,128)(2,1)}) %all-gather.2.cloned.1.call-update) | async-done | bytes 4194320 | tf_op jit(solution)/shard_map/all_gather | solution.py:86
  78.2 26.6 %while.15 = (s32[]{:T(128)}, f32[16,4,32]{2,1,0:T(4,128)S(1)}, f32[16,4,32]{2,1,0:T(4,128)S(1)}, f32[16,32,4,32]{1,3,2,0:T(8,128)S(1)}, bf16[2,16,512,128]{3,2,0...) while((s32[]{:T(128)}, f32[16,4,32]{2,1,0:T(4,128)S(1)}, ...), condition=%wide.region_5.6_spmd.clone, body=%wide.region_2.5_spmd.clone.sunk | while | flops 684996096 | bytes 52896580 | solution.py:62
  78.2 0.6 dynamic_slice.24
  79.4 0.7 fusion.63
  80.1 0.0 copy-done.3
  80.1 2.9 %convolution_convert_fusion.3 = bf16[16,512,256]{1,2,0:T(8,128)(2,1)S(1)} fusion(bf16[2,16,512,128]{3,2,0,1:T(8,128)(2,1)} %get-tuple-element.254, s32[]{:T(128)} %get-tuple-element.236, bf16[128,256]{0,1:T(8,128)(2,1)} %get-tuple-element.255), kind=kOutput, calls=%fused_computation.6.clone.1 | convolution fusion | flops 538968064 | bytes 6357504 | tf_op jit(solution)/shard_map/while/body/eval_jaxpr/dot_general | solution.py:28
  82.9 0.0 copy-start.2
  83.0 0.3 fusion.64
  83.3 0.7 copy-done.2
  84.0 2.7 %fusion.65 = (f32[16,4,32]{2,1,0:T(4,128)S(1)}, f32[16,4,512,32]{2,3,1,0:T(8,128)}) fusion(f32[512]{0:T(512)S(1)} %fusion.63, f32[4,32,512]{2,1,0:T(8,128)S(1)} %dynamic-slice_convert_fusion.2, bf16[16,32,4,32]{3,1,2,0:T(8,128)(2,1)S(1)} %copy-done.2, bf16[16,512,4,32]{1,3,2,0:T(8,128)(2,1)S(1)} %bitcast.90), kind=kOutput, calls=%fused_computation.5.clone.1 | convolution fusion | flops 70252544 | bytes 6694912 | tf_op jit(solution)/shard_map/while/body/eval_jaxpr/rjhd,rkhd->rhjk/dot_general | solution.py:32
  86.8 3.4 %fusion.69 = f32[16,32,4,32]{1,3,2,0:T(8,128)S(1)} fusion(bf16[16,512,4,32]{1,3,2,0:T(8,128)(2,1)S(1)} %bitcast.89, f32[16,4,512,32]{2,3,1,0:T(8,128)} %get-tuple-element.219, f32[16,4,32]{2,1,0:T(4,128)S(1)} %get-tuple-element.251, f32[512]{0:T(512)S(1)} %fusion.63, f32[4,32,512]{2,1,0:T(8,128)S(1)} %dynamic-slice_convert_fusion.2, ...), kind=kOutput, calls=%fused_computation.14.clone.1 | convolution fusion | flops 71499776 | bytes 7096321 | tf_op jit(solution)/shard_map/while/body/eval_jaxpr/rhjk,rkhd->rjhd/dot_general | solution.py:44
  90.2 0.0 copy-done.1
  90.2 1.2 %fusion.67 = f32[16,4,32]{2,1,0:T(4,128)S(1)} fusion(f32[16,4,512,32]{2,3,1,0:T(8,128)S(1)} %copy-done.1, f32[16,4,32]{2,1,0:T(4,128)S(1)} %get-tuple-element.251, f32[512]{0:T(512)S(1)} %fusion.63, f32[4,32,512]{2,1,0:T(8,128)S(1)} %dynamic-slice_convert_fusion.2), kind=kLoop, calls=%fused_computation.4.clone.1 | loop fusion | flops 4192256 | bytes 4474880 | tf_op jit(solution)/shard_map/while/body/eval_jaxpr/reduce_sum | solution.py:42
  91.4 0.1 fusion.68
  91.5 0.0 copy-start.3
  91.5 0.6 dynamic_slice.24
  92.7 0.7 fusion.63
  93.4 2.9 %convolution_convert_fusion.3 = bf16[16,512,256]{1,2,0:T(8,128)(2,1)S(1)} fusion(bf16[2,16,512,128]{3,2,0,1:T(8,128)(2,1)} %get-tuple-element.254, s32[]{:T(128)} %get-tuple-element.236, bf16[128,256]{0,1:T(8,128)(2,1)} %get-tuple-element.255), kind=kOutput, calls=%fused_computation.6.clone.1 | convolution fusion | flops 538968064 | bytes 6357504 | tf_op jit(solution)/shard_map/while/body/eval_jaxpr/dot_general | solution.py:28
  96.2 0.3 fusion.64
  96.6 0.7 copy-done.2
  97.3 2.8 %fusion.65 = (f32[16,4,32]{2,1,0:T(4,128)S(1)}, f32[16,4,512,32]{2,3,1,0:T(8,128)}) fusion(f32[512]{0:T(512)S(1)} %fusion.63, f32[4,32,512]{2,1,0:T(8,128)S(1)} %dynamic-slice_convert_fusion.2, bf16[16,32,4,32]{3,1,2,0:T(8,128)(2,1)S(1)} %copy-done.2, bf16[16,512,4,32]{1,3,2,0:T(8,128)(2,1)S(1)} %bitcast.90), kind=kOutput, calls=%fused_computation.5.clone.1 | convolution fusion | flops 70252544 | bytes 6694912 | tf_op jit(solution)/shard_map/while/body/eval_jaxpr/rjhd,rkhd->rhjk/dot_general | solution.py:32
  100.1 3.4 %fusion.69 = f32[16,32,4,32]{1,3,2,0:T(8,128)S(1)} fusion(bf16[16,512,4,32]{1,3,2,0:T(8,128)(2,1)S(1)} %bitcast.89, f32[16,4,512,32]{2,3,1,0:T(8,128)} %get-tuple-element.219, f32[16,4,32]{2,1,0:T(4,128)S(1)} %get-tuple-element.251, f32[512]{0:T(512)S(1)} %fusion.63, f32[4,32,512]{2,1,0:T(8,128)S(1)} %dynamic-slice_convert_fusion.2, ...), kind=kOutput, calls=%fused_computation.14.clone.1 | convolution fusion | flops 71499776 | bytes 7096321 | tf_op jit(solution)/shard_map/while/body/eval_jaxpr/rhjk,rkhd->rjhd/dot_general | solution.py:44
  103.5 0.0 copy-done.1
  103.5 1.2 %fusion.67 = f32[16,4,32]{2,1,0:T(4,128)S(1)} fusion(f32[16,4,512,32]{2,3,1,0:T(8,128)S(1)} %copy-done.1, f32[16,4,32]{2,1,0:T(4,128)S(1)} %get-tuple-element.251, f32[512]{0:T(512)S(1)} %fusion.63, f32[4,32,512]{2,1,0:T(8,128)S(1)} %dynamic-slice_convert_fusion.2), kind=kLoop, calls=%fused_computation.4.clone.1 | loop fusion | flops 4192256 | bytes 4474880 | tf_op jit(solution)/shard_map/while/body/eval_jaxpr/reduce_sum | solution.py:42
  104.7 0.1 fusion.68
  104.8 0.0 copy-done.4
  104.8 0.2 broadcast_divide_fusion
  105.0 0.3 copy.23
  105.3 1.9 %convolution_convert_fusion.1 = bf16[16,32,128]{2,1,0:T(8,128)(2,1)} fusion(f32[16,32,128]{2,1,0:T(8,128)S(1)} %copy.23, bf16[16,32,128]{2,1,0:T(8,128)(2,1)} %fusion.31, bf16[128,128]{1,0:T(8,128)(2,1)} %param.13, bf16[128,128]{1,0:T(8,128)(2,1)} %param.12), kind=kOutput, calls=%fused_computation.34 | convolution fusion | flops 33947648 | bytes 589824 | tf_op jit(solution)/shard_map/dot_general | solution.py:75
  (21 shorter events, 0.1 us)
Async XLA Ops:
  6.5 14.7 %copy-start = (bf16[128,128]{1,0:T(8,128)(2,1)S(1)}, bf16[128,128]{1,0:T(8,128)(2,1)}, u32[]{:S(2)}) copy-start(bf16[128,128]{1,0:T(8,128)(2,1)} %param.10) | copy-start | bytes 98308
  6.5 17.0 %copy-start.5 = (bf16[128,256]{1,0:T(8,128)(2,1)S(1)}, bf16[128,256]{1,0:T(8,128)(2,1)}, u32[]{:S(2)}) copy-start(bf16[128,256]{1,0:T(8,128)(2,1)} %param.11) | copy-start | bytes 196612
  6.5 71.7 %all-gather.2.cloned.1.call-start = ((), (), s32[]{:S(2)}) async-start(), calls=%async_computation.1 | async-start | bytes 4325376 | tf_op jit(solution)/shard_map/all_gather | solution.py:86
  13.9 19.3 %all-to-all-start = ((bf16[32,2,2048]{2,1,0:T(2,128)(2,1)}), bf16[32,2,2048]{2,1,0:T(2,128)(2,1)S(1)}, u32[]{:S(2)}, u32[]{:S(2)}) async-start(bf16[32,2,2048]{2,1,0:T(2,128)(2,1)} %reshape.48), calls=%async_computation | async-start | bytes 524288 | tf_op jit(solution)/shard_map/all_to_all | solution.py:81
  78.2 1.9 %copy-start.3 = (bf16[4,32,1024]{2,1,0:T(8,128)(2,1)}, bf16[4,32,1024]{2,1,0:T(8,128)(2,1)S(1)}, u32[]{:S(2)}) copy-start(bf16[4,32,1024]{2,1,0:T(8,128)(2,1)S(1)} %get-tuple-element.258) | copy-start | bytes 786436 | tf_op jit(solution)/shard_map/while
  82.9 1.0 copy-start.2
  86.8 3.5 %copy-start.1 = (f32[16,4,512,32]{2,3,1,0:T(8,128)S(1)}, f32[16,4,512,32]{2,3,1,0:T(8,128)}, u32[]{:S(2)}) copy-start(f32[16,4,512,32]{2,3,1,0:T(8,128)} %get-tuple-element.219) | copy-start | bytes 12582916 | tf_op jit(solution)/shard_map/while
  90.2 1.3 %copy-start.4 = (bf16[4,32,1024]{2,1,0:T(8,128)(2,1)S(1)}, bf16[4,32,1024]{2,1,0:T(8,128)(2,1)}, u32[]{:S(2)}) copy-start(bf16[4,32,1024]{2,1,0:T(8,128)(2,1)} %copy-done.3) | copy-start | bytes 786436 | tf_op jit(solution)/shard_map/while
  91.5 1.9 %copy-start.3 = (bf16[4,32,1024]{2,1,0:T(8,128)(2,1)}, bf16[4,32,1024]{2,1,0:T(8,128)(2,1)S(1)}, u32[]{:S(2)}) copy-start(bf16[4,32,1024]{2,1,0:T(8,128)(2,1)S(1)} %get-tuple-element.258) | copy-start | bytes 786436 | tf_op jit(solution)/shard_map/while
  96.2 1.0 copy-start.2
  100.1 3.5 %copy-start.1 = (f32[16,4,512,32]{2,3,1,0:T(8,128)S(1)}, f32[16,4,512,32]{2,3,1,0:T(8,128)}, u32[]{:S(2)}) copy-start(f32[16,4,512,32]{2,3,1,0:T(8,128)} %get-tuple-element.219) | copy-start | bytes 12582916 | tf_op jit(solution)/shard_map/while
  103.5 1.3 %copy-start.4 = (bf16[4,32,1024]{2,1,0:T(8,128)(2,1)S(1)}, bf16[4,32,1024]{2,1,0:T(8,128)(2,1)}, u32[]{:S(2)}) copy-start(bf16[4,32,1024]{2,1,0:T(8,128)(2,1)} %copy-done.3) | copy-start | bytes 786436 | tf_op jit(solution)/shard_map/while
Sparse Core Ops, SparseCore 0:
  10.7 67.4 all-gather.1
where the time goes:
time: 115 us; the launch traced here: 114 us
  waiting for transfers between devices  51.7 us (45%)
  matrix products  21.1 us (18%)
  between operations  13.5 us (12%)
  local copies, waits for them, and re-layouts  11.1 us (10%)
  other arithmetic  8.07 us (7%)
  starting transfers between devices  7.33 us (6%)
  loops' own time  1.32 us (1%)
    all_gather x1, waiting for transfers between devices, gather_keys(): lax.all_gather(normed, 'col', axis=1, tiled=True)  42.7 us
    all_to_all x1, waiting for transfers between devices, on_device(): lax.all_to_all(pair_bias, 'col', split_axis=2, concat_axis=1, tiled=True)  8.93 us
    all_to_all x1, starting transfers between devices, on_device(): lax.all_to_all(pair_bias, 'col', split_axis=2, concat_axis=1, tiled=True)  7.33 us
    dot_general x2, matrix products, consume(): jnp.einsum('rhjk,rkhd->rjhd', weights, value_tile, preferred_element_type...  6.85 us
    dot_general x2, matrix products, consume(): jnp.dot(segment, w_kv, preferred_element_type=jnp.float32)  5.72 us
    dot_general x2, matrix products, consume(): jnp.einsum('rjhd,rkhd->rhjk', queries, key_tile, preferred_element_type=j...  5.51 us
    unnamed x9, local copies, waits for them, and re-layouts  5.47 us
    reduce_sum x2, other arithmetic, consume(): new_sum = run_sum * rescale + jnp.sum(expon, axis=-1)  2.38 us
  transfers between devices with their start and end apart: 2, of which 2 were waited for; matrix products, arithmetic and copies ran while one was open for 7% of the time, Pallas kernels for 0%

commit v1 on v0

--- a/solution.py
+++ b/solution.py
@@ -4,6 +4,28 @@
 from jax.sharding import PartitionSpec as P
 
 HEADS = 4
+
+
+def in_order(blocks, dim):
+    shape = list(blocks.shape[1:])
+    shape[dim] *= blocks.shape[0]
+    return jnp.moveaxis(blocks, 0, dim).reshape(shape)
+
+
+def collected_by_bits(value, axis):
+    devices = lax.axis_size(axis)
+    pieces = value[None]
+    for level in range(devices.bit_length() - 1):
+        distance = 1 << level
+        partner_block = lax.ppermute(pieces, axis, [(i, i ^ distance) for i in range(devices)])
+        both = jnp.stack([pieces, partner_block])
+        upper = lax.axis_index(axis) >> level & 1
+        pieces = jnp.where(upper == 0, both, both[::-1]).reshape(-1, *value.shape)
+    return pieces
+
+
+def doubled_up(shard, axis, dim):
+    return in_order(collected_by_bits(shard, axis), dim)
 
 
 def normalize(pair_block):
@@ -82,9 +104,7 @@
     bias_query = jnp.transpose(received, (0, 2, 1))
 
     def gather_keys(fold_piece, initial):
-        return fold_piece(
-            initial, lax.all_gather(normed, "col", axis=1, tiled=True), jnp.int32(0), True
-        )
+        return fold_piece(initial, doubled_up(normed, "col", 1), jnp.int32(0), True)
 
     return attend(normed, bias_query, key_limit, w_query, w_kv, w_gate, w_out, gather_keys)
 

time: 115 us -> 195 us (1.70)
  waiting for transfers between devices: 51.7 us -> 125 us
  between operations: 13.5 us -> 0.23 us
  local copies, waits for them, and re-layouts: 11.1 us -> 20 us
  other arithmetic: 8.07 us -> 14.6 us
  starting transfers between devices: 7.33 us -> 13.4 us
    all_to_all x1, waiting for transfers between devices: 8.93 us -> 83.1 us  [on_device(): lax.all_to_all(pair_bias, 'col', split_axis=2, concat_axis=1, tiled=True)]
    all_gather x1 -> x0, waiting for transfers between devices: 42.7 us -> none  [gather_keys(): lax.all_gather(normed, 'col', axis=1, tiled=True)]
    ppermute x0 -> x5, waiting for transfers between devices: none -> 41.5 us  [collected_by_bits(): lax.ppermute(pieces, axis, [(i, i ^ distance) for i in range(devices)])]
    ppermute x0 -> x5, starting transfers between devices: none -> 9.25 us  [collected_by_bits(): lax.ppermute(pieces, axis, [(i, i ^ distance) for i in range(devices)])]
    select_n x0 -> x4, other arithmetic: none -> 4.41 us  [collected_by_bits(): pieces = jnp.where(upper == 0, both, both[::-1]).reshape(-1, *value.shape)]
    unnamed x9 -> x13, local copies, waits for them, and re-layouts: 5.47 us -> 9.85 us
    another operation x0 -> x7, other arithmetic: none -> 3.91 us  [collected_by_bits(): both = jnp.stack([pieces, partner_block])]
    all_to_all x2, local copies, waits for them, and re-layouts: 1.77 us -> 5.21 us  [on_device(): lax.all_to_all(pair_bias, 'col', split_axis=2, concat_axis=1, tiled=True)]
  transfers between devices with their start and end apart: 2 -> 6, of which waited for: 2 -> 5; matrix products, arithmetic and copies ran while one was open for 7% -> 7% of each run, Pallas kernels for 0% -> 0%
where the time goes in v1:
time: 195 us
  waiting for transfers between devices  125 us (64%)
  matrix products  20.4 us (10%)
  local copies, waits for them, and re-layouts  20 us (10%)
  other arithmetic  14.6 us (7%)
  starting transfers between devices  13.4 us (7%)
    all_to_all x1, waiting for transfers between devices, on_device(): lax.all_to_all(pair_bias, 'col', split_axis=2, concat_axis=1, tiled=True)  83.1 us
    ppermute x5, waiting for transfers between devices, collected_by_bits(): lax.ppermute(pieces, axis, [(i, i ^ distance) for i in range(devices)])  41.5 us
    unnamed x13, local copies, waits for them, and re-layouts  9.85 us
    ppermute x5, starting transfers between devices, collected_by_bits(): lax.ppermute(pieces, axis, [(i, i ^ distance) for i in range(devices)])  9.25 us
    dot_general x2, matrix products, consume(): jnp.einsum('rhjk,rkhd->rjhd', weights, value_tile, preferred_element_type...  6.86 us
    dot_general x2, matrix products, consume(): jnp.dot(segment, w_kv, preferred_element_type=jnp.float32)  5.71 us
    dot_general x2, matrix products, consume(): jnp.einsum('rjhd,rkhd->rhjk', queries, key_tile, preferred_element_type=j...  5.49 us
    all_to_all x2, local copies, waits for them, and re-layouts, on_device(): lax.all_to_all(pair_bias, 'col', split_axis=2, concat_axis=1, tiled=True)  5.21 us
  transfers between devices with their start and end apart: 6, of which 5 were waited for; matrix products, arithmetic and copies ran while one was open for 7% of the time, Pallas kernels for 0%

profile of v1, /device:TPU:0, one launch (start us, length us, event | category | flops | bytes accessed | tf_op | source)
XLA Modules:
  0.0 194.8 jit_solution(13374826686227610735)
XLA Ops:
  0.0 1.0 convert_reduce_fusion
  1.1 1.2 fusion.30
  2.3 1.1 fusion.41
  3.4 0.6 collective-permute-start
  3.9 1.0 collective-permute-done
  5.0 2.9 %collective-permute-start.1 = (bf16[2,16,32,128]{3,2,1,0:T(8,128)(2,1)S(1)}, bf16[2,16,32,128]{3,2,1,0:T(8,128)(2,1)S(1)}, u32[]{:S(2)}, u32[]{:S(2)}) collective-permute-start(bf16[2,16,32,128]{3,2,1,0:T(8,128)(2,1)S(1)} %get-tuple-element.150), channel_id=1, source_target_pairs={{0,2},{1,3},{2,0},{3,1},{4,6},{5,7},{6,4},{7,5},{8,10},{9,11},{10,... | collective-permute-start | bytes 786440 | tf_op jit(solution)/shard_map/ppermute | solution.py:20
  7.9 6.6 %collective-permute-done.1 = bf16[2,16,32,128]{3,2,1,0:T(8,128)(2,1)S(1)} collective-permute-done((bf16[2,16,32,128]{3,2,1,0:T(8,128)(2,1)S(1)}, bf16[2,16,32,128]{3,2,1,0:T(8,128)(2,1)S(1)}, u32[]{:S(2)}, u32[]{:S(2)}) %collective-permute-start.1) | collective-permute-done | bytes 262176 | tf_op jit(solution)/shard_map/ppermute | solution.py:20
  14.7 1.8 collective-permute-start.2
  16.6 11.6 %collective-permute-done.2 = bf16[4,16,32,128]{3,2,1,0:T(8,128)(2,1)S(1)} collective-permute-done((bf16[4,16,32,128]{3,2,1,0:T(8,128)(2,1)S(1)}, bf16[4,16,32,128]{3,2,1,0:T(8,128)(2,1)S(1)}, u32[]{:S(2)}, u32[]{:S(2)}) %collective-permute-start.2) | collective-permute-done | bytes 524320 | tf_op jit(solution)/shard_map/ppermute | solution.py:20
  28.3 0.2 reverse_select_fusion.2
  28.6 1.6 collective-permute-start.3
  30.2 22.2 %collective-permute-done.3 = bf16[8,16,32,128]{3,2,0,1:T(8,128)(2,1)S(1)} collective-permute-done((bf16[8,16,32,128]{3,2,0,1:T(8,128)(2,1)S(1)}, bf16[8,16,32,128]{3,2,0,1:T(8,128)(2,1)S(1)}, u32[]{:S(2)}, u32[]{:S(2)}) %collective-permute-start.3) | collective-permute-done | bytes 1048608 | tf_op jit(solution)/shard_map/ppermute | solution.py:20
  52.5 0.6 pad_maximum_fusion.1
  53.1 0.7 reverse_select_fusion.1
  53.8 2.3 %collective-permute-start.4 = (bf16[16,16,32,128]{3,2,0,1:T(8,128)(2,1)S(1)}, bf16[16,16,32,128]{3,2,0,1:T(8,128)(2,1)}, u32[]{:S(2)}, u32[]{:S(2)}) collective-permute-start(bf16[16,16,32,128]{3,2,0,1:T(8,128)(2,1)S(1)} %bitcast.121), channel_id=1, source_target_pairs={{0,16},{1,17},{2,18},{3,19},{4,20},{5,21},{6,22},{7,23},{8,24},{9,... | collective-permute-start | bytes 6291464 | tf_op jit(solution)/shard_map/ppermute | solution.py:20
  56.1 1.6 copy.21
  57.7 1.7 reshape.64
  59.4 4.1 %all-to-all-start = ((bf16[32,2,2048]{2,1,0:T(2,128)(2,1)}), bf16[32,2,2048]{2,1,0:T(2,128)(2,1)}, u32[]{:S(2)}, u32[]{:S(2)}) async-start(bf16[32,2,2048]{2,1,0:T(2,128)(2,1)} %reshape.64), calls=%async_computation | async-start | bytes 524288 | tf_op jit(solution)/shard_map/all_to_all | solution.py:103
  63.6 0.3 fusion.27
  63.9 1.1 reshape.56
  65.0 2.0 %copy.25 = bf16[16,32,4,32]{3,1,2,0:T(8,128)(2,1)} copy(bf16[16,32,4,32]{3,2,1,0:T(4,128)(2,1)} %reshape.56) | data formatting | bytes 262144
  67.0 1.6 copy.24
  68.5 83.1 %all-to-all-done = bf16[32,2,2048]{2,1,0:T(2,128)(2,1)} async-done(((bf16[32,2,2048]{2,1,0:T(2,128)(2,1)}), bf16[32,2,2048]{2,1,0:T(2,128)(2,1)}, u32[]{:S(2)}, u32[]{:S(2)}) %all-to-all-start) | async-done | bytes 262176 | tf_op jit(solution)/shard_map/all_to_all | solution.py:103
  151.6 3.0 %reshape.65 = bf16[1024,4,32]{2,1,0:T(4,128)(2,1)} reshape(bf16[32,2,2048]{2,1,0:T(2,128)(2,1)} %all-to-all-done) | data formatting | bytes 524288
  154.6 2.9 %copy.22 = bf16[4,32,32,32]{2,1,3,0:T(8,128)(2,1)} copy(bf16[4,32,32,32]{2,0,3,1:T(4,128)(2,1)} %bitcast.125) | data formatting | bytes 524288 | tf_op jit(solution)/shard_map/all_to_all | solution.py:103
  157.5 2.3 %all_to_all.16 = bf16[4,1024,32]{1,2,0:T(8,128)(2,1)S(1)} reshape(bf16[4,32,32,32]{2,1,3,0:T(8,128)(2,1)} %copy.22) | data formatting | bytes 524288 | tf_op jit(solution)/shard_map/all_to_all | solution.py:103
  159.9 2.0 %pad_maximum_fusion = bf16[2,16,16,32,128]{4,3,1,0,2:T(8,128)(2,1)S(1)} fusion(bf16[1,16,16,32,128]{4,3,1,0,2:T(8,128)(2,1)} %bitcast.15, bf16[1,16,16,32,128]{4,3,1,0,2:T(8,128)(2,1)S(1)} %bitcast.122), kind=kLoop, calls=%fused_computation.27 | loop fusion | flops 2097152 | bytes 8388608 | tf_op jit(solution)/shard_map/stack | solution.py:21
  161.9 3.4 %reverse_select_fusion = bf16[2,16,16,32,128]{4,3,1,0,2:T(8,128)(2,1)} fusion(bf16[2,16,16,32,128]{4,3,1,0,2:T(8,128)(2,1)S(1)} %pad_maximum_fusion, pred[]{:T(512)S(6)} %eq.15), kind=kLoop, calls=%fused_computation.26 | loop fusion | flops 2097152 | bytes 8388609 | tf_op jit(solution)/shard_map/jit(_where)/select_n | solution.py:23
  165.3 27.0 %while.15 = (s32[]{:T(128)}, f32[16,4,32]{2,1,0:T(4,128)S(1)}, f32[16,4,32]{2,1,0:T(4,128)S(1)}, f32[16,32,4,32]{1,3,2,0:T(8,128)S(1)}, bf16[2,16,512,128]{3,2,0...) while((s32[]{:T(128)}, f32[16,4,32]{2,1,0:T(4,128)S(1)}, ...), condition=%wide.region_5.6_spmd.clone, body=%wide.region_2.5_spmd.clone.sunk | while | flops 684996096 | bytes 53158760 | solution.py:84
  165.3 0.7 dynamic_slice.24
  166.7 0.7 fusion.70
  167.3 2.9 %convolution_convert_fusion.3 = bf16[16,512,256]{1,2,0:T(8,128)(2,1)S(1)} fusion(bf16[2,16,512,128]{3,2,0,1:T(8,128)(2,1)} %get-tuple-element.258, s32[]{:T(128)} %get-tuple-element.240, bf16[128,256]{0,1:T(8,128)(2,1)S(1)} %get-tuple-element.259), kind=kOutput, calls=%fused_computation.6.clone.1 | convolution fusion | flops 538968064 | bytes 6357504 | tf_op jit(solution)/shard_map/while/body/eval_jaxpr/dot_general | solution.py:50
  170.2 0.3 fusion.71
  170.5 0.7 copy-done.2
  171.2 2.7 %fusion.72 = (f32[16,4,32]{2,1,0:T(4,128)S(1)}, f32[16,4,512,32]{2,3,1,0:T(8,128)}) fusion(f32[512]{0:T(512)S(1)} %fusion.70, f32[4,32,512]{2,1,0:T(8,128)S(1)} %dynamic-slice_convert_fusion.2, bf16[16,32,4,32]{3,1,2,0:T(8,128)(2,1)S(1)} %copy-done.2, bf16[16,512,4,32]{1,3,2,0:T(8,128)(2,1)S(1)} %bitcast.117), kind=kOutput, calls=%fused_computation.5.clone.1 | convolution fusion | flops 70252544 | bytes 6694912 | tf_op jit(solution)/shard_map/while/body/eval_jaxpr/rjhd,rkhd->rhjk/dot_general | solution.py:54
  174.0 3.4 %fusion.76 = f32[16,32,4,32]{1,3,2,0:T(8,128)S(1)} fusion(bf16[16,512,4,32]{1,3,2,0:T(8,128)(2,1)S(1)} %bitcast.116, f32[16,4,512,32]{2,3,1,0:T(8,128)} %get-tuple-element.223, f32[16,4,32]{2,1,0:T(4,128)S(1)} %get-tuple-element.255, f32[512]{0:T(512)S(1)} %fusion.70, f32[4,32,512]{2,1,0:T(8,128)S(1)} %dynamic-slice_convert_fusion.2, ...), kind=kOutput, calls=%fused_computation.14.clone.1 | convolution fusion | flops 71499776 | bytes 7096321 | tf_op jit(solution)/shard_map/while/body/eval_jaxpr/rhjk,rkhd->rjhd/dot_general | solution.py:66
  177.5 1.2 fusion.74
  178.8 0.7 dynamic_slice.24
  180.2 0.7 fusion.70
  180.8 2.9 %convolution_convert_fusion.3 = bf16[16,512,256]{1,2,0:T(8,128)(2,1)S(1)} fusion(bf16[2,16,512,128]{3,2,0,1:T(8,128)(2,1)} %get-tuple-element.258, s32[]{:T(128)} %get-tuple-element.240, bf16[128,256]{0,1:T(8,128)(2,1)S(1)} %get-tuple-element.259), kind=kOutput, calls=%fused_computation.6.clone.1 | convolution fusion | flops 538968064 | bytes 6357504 | tf_op jit(solution)/shard_map/while/body/eval_jaxpr/dot_general | solution.py:50
  183.7 0.3 fusion.71
  184.0 0.7 copy-done.2
  184.8 2.7 %fusion.72 = (f32[16,4,32]{2,1,0:T(4,128)S(1)}, f32[16,4,512,32]{2,3,1,0:T(8,128)}) fusion(f32[512]{0:T(512)S(1)} %fusion.70, f32[4,32,512]{2,1,0:T(8,128)S(1)} %dynamic-slice_convert_fusion.2, bf16[16,32,4,32]{3,1,2,0:T(8,128)(2,1)S(1)} %copy-done.2, bf16[16,512,4,32]{1,3,2,0:T(8,128)(2,1)S(1)} %bitcast.117), kind=kOutput, calls=%fused_computation.5.clone.1 | convolution fusion | flops 70252544 | bytes 6694912 | tf_op jit(solution)/shard_map/while/body/eval_jaxpr/rjhd,rkhd->rhjk/dot_general | solution.py:54
  187.5 3.4 %fusion.76 = f32[16,32,4,32]{1,3,2,0:T(8,128)S(1)} fusion(bf16[16,512,4,32]{1,3,2,0:T(8,128)(2,1)S(1)} %bitcast.116, f32[16,4,512,32]{2,3,1,0:T(8,128)} %get-tuple-element.223, f32[16,4,32]{2,1,0:T(4,128)S(1)} %get-tuple-element.255, f32[512]{0:T(512)S(1)} %fusion.70, f32[4,32,512]{2,1,0:T(8,128)S(1)} %dynamic-slice_convert_fusion.2, ...), kind=kOutput, calls=%fused_computation.14.clone.1 | convolution fusion | flops 71499776 | bytes 7096321 | tf_op jit(solution)/shard_map/while/body/eval_jaxpr/rhjk,rkhd->rjhd/dot_general | solution.py:66
  191.0 1.2 fusion.74
  192.3 0.2 broadcast_divide_fusion
  192.5 0.3 copy.27
  192.8 2.0 %convolution_convert_fusion.1 = bf16[16,32,128]{2,1,0:T(8,128)(2,1)} fusion(f32[16,32,128]{2,1,0:T(8,128)S(1)} %copy.27, bf16[128,128]{1,0:T(8,128)(2,1)} %param.13, bf16[128,128]{1,0:T(8,128)(2,1)} %param.12, bf16[16,32,128]{2,1,0:T(8,128)(2,1)} %param.9, f32[16,32]{1,0:T(8,128)} %copy-done.8, f32[16,32]{1,0:T(8,128)S(1)} %broadcast_multiply_fusion), kind=kOutput, calls=%fused_computation.39 | convolution fusion | flops 34209792 | bytes 593920 | tf_op jit(solution)/shard_map/dot_general | solution.py:97
  (47 shorter events, 0.8 us)
Async XLA Ops:
  0.0 63.6 %copy-start = (bf16[128,128]{1,0:T(8,128)(2,1)S(1)}, bf16[128,128]{1,0:T(8,128)(2,1)}, u32[]{:S(2)}) copy-start(bf16[128,128]{1,0:T(8,128)(2,1)} %param.10) | copy-start | bytes 98308
  2.2 61.3 %copy-start.8 = (f32[16,32]{1,0:T(8,128)}, f32[16,32]{1,0:T(8,128)S(1)}, u32[]{:S(2)}) copy-start(f32[16,32]{1,0:T(8,128)S(1)} %add_rsqrt_fusion) | copy-start | bytes 6148
  3.4 1.5 collective-permute-start
  5.0 9.5 %collective-permute-start.1 = (bf16[2,16,32,128]{3,2,1,0:T(8,128)(2,1)S(1)}, bf16[2,16,32,128]{3,2,1,0:T(8,128)(2,1)S(1)}, u32[]{:S(2)}, u32[]{:S(2)}) collective-permute-start(bf16[2,16,32,128]{3,2,1,0:T(8,128)(2,1)S(1)} %get-tuple-element.150), channel_id=1, source_target_pairs={{0,2},{1,3},{2,0},{3,1},{4,6},{5,7},{6,4},{7,5},{8,10},{9,11},{10,... | collective-permute-start | bytes 786440 | tf_op jit(solution)/shard_map/ppermute | solution.py:20
  14.7 13.5 %collective-permute-start.2 = (bf16[4,16,32,128]{3,2,1,0:T(8,128)(2,1)S(1)}, bf16[4,16,32,128]{3,2,1,0:T(8,128)(2,1)S(1)}, u32[]{:S(2)}, u32[]{:S(2)}) collective-permute-start(bf16[4,16,32,128]{3,2,1,0:T(8,128)(2,1)S(1)} %bitcast.127), channel_id=1, source_target_pairs={{0,4},{1,5},{2,6},{3,7},{4,0},{5,1},{6,2},{7,3},{8,12},{9,13},{10,... | collective-permute-start | bytes 1572872 | tf_op jit(solution)/shard_map/ppermute | solution.py:20
  28.6 23.8 %collective-permute-start.3 = (bf16[8,16,32,128]{3,2,0,1:T(8,128)(2,1)S(1)}, bf16[8,16,32,128]{3,2,0,1:T(8,128)(2,1)S(1)}, u32[]{:S(2)}, u32[]{:S(2)}) collective-permute-start(bf16[8,16,32,128]{3,2,0,1:T(8,128)(2,1)S(1)} %copy.19), channel_id=1, source_target_pairs={{0,8},{1,9},{2,10},{3,11},{4,12},{5,13},{6,14},{7,15},{8,0},{9,1},... | collective-permute-start | bytes 3145736 | tf_op jit(solution)/shard_map/ppermute | solution.py:20
  53.1 10.5 %copy-start.7 = (bf16[16,32,128]{2,1,0:T(8,128)(2,1)S(1)}, bf16[16,32,128]{2,1,0:T(8,128)(2,1)}, u32[]{:S(2)}) copy-start(bf16[16,32,128]{2,1,0:T(8,128)(2,1)} %param.9) | copy-start | bytes 393220
  53.8 106.1 %collective-permute-start.4 = (bf16[16,16,32,128]{3,2,0,1:T(8,128)(2,1)S(1)}, bf16[16,16,32,128]{3,2,0,1:T(8,128)(2,1)}, u32[]{:S(2)}, u32[]{:S(2)}) collective-permute-start(bf16[16,16,32,128]{3,2,0,1:T(8,128)(2,1)S(1)} %bitcast.121), channel_id=1, source_target_pairs={{0,16},{1,17},{2,18},{3,19},{4,20},{5,21},{6,22},{7,23},{8,24},{9,... | collective-permute-start | bytes 6291464 | tf_op jit(solution)/shard_map/ppermute | solution.py:20
  59.4 92.3 %all-to-all-start = ((bf16[32,2,2048]{2,1,0:T(2,128)(2,1)}), bf16[32,2,2048]{2,1,0:T(2,128)(2,1)}, u32[]{:S(2)}, u32[]{:S(2)}) async-start(bf16[32,2,2048]{2,1,0:T(2,128)(2,1)} %reshape.64), calls=%async_computation | async-start | bytes 524288 | tf_op jit(solution)/shard_map/all_to_all | solution.py:103
  161.9 3.4 %copy-start.5 = (bf16[128,256]{0,1:T(8,128)(2,1)S(1)}, bf16[128,256]{0,1:T(8,128)(2,1)}, u32[]{:S(2)}) copy-start(bf16[128,256]{0,1:T(8,128)(2,1)} %copy.24) | copy-start | bytes 196612
  165.3 2.1 %copy-start.3 = (bf16[4,32,1024]{2,1,0:T(8,128)(2,1)}, bf16[4,32,1024]{2,1,0:T(8,128)(2,1)S(1)}, u32[]{:S(2)}) copy-start(bf16[4,32,1024]{2,1,0:T(8,128)(2,1)S(1)} %get-tuple-element.262) | copy-start | bytes 786436 | tf_op jit(solution)/shard_map/while
  170.2 1.0 copy-start.2
  174.0 3.5 %copy-start.1 = (f32[16,4,512,32]{2,3,1,0:T(8,128)S(1)}, f32[16,4,512,32]{2,3,1,0:T(8,128)}, u32[]{:S(2)}) copy-start(f32[16,4,512,32]{2,3,1,0:T(8,128)} %get-tuple-element.223) | copy-start | bytes 12582916 | tf_op jit(solution)/shard_map/while
  177.5 1.3 copy-start.4
  177.5 1.3 copy-start.6
  178.8 2.1 %copy-start.3 = (bf16[4,32,1024]{2,1,0:T(8,128)(2,1)}, bf16[4,32,1024]{2,1,0:T(8,128)(2,1)S(1)}, u32[]{:S(2)}) copy-start(bf16[4,32,1024]{2,1,0:T(8,128)(2,1)S(1)} %get-tuple-element.262) | copy-start | bytes 786436 | tf_op jit(solution)/shard_map/while
  183.7 1.0 copy-start.2
  187.5 3.5 %copy-start.1 = (f32[16,4,512,32]{2,3,1,0:T(8,128)S(1)}, f32[16,4,512,32]{2,3,1,0:T(8,128)}, u32[]{:S(2)}) copy-start(f32[16,4,512,32]{2,3,1,0:T(8,128)} %get-tuple-element.223) | copy-start | bytes 12582916 | tf_op jit(solution)/shard_map/while
  191.0 1.3 copy-start.4
  191.0 1.3 copy-start.6
